TPU v7x, 32 devices: a whole 2x2x4 slice. The times are simulated.
32 devices in a mesh: row: 4 (over x, core), col: 8 (over z, y).
Axes of the slice: x: 2, y: 2, z: 4, core: 2. Of those that a mesh axis runs over, the one named last changes fastest.
Arguments:
- pair_density: bfloat16 [2048, 8192], P('col', 'row'), may hold values from -6 to 6
- scale_exp: int32 [2048], replicated, may hold values from -1 to 1
- pair_weight: int32 [2048], replicated, may hold values from 1 to 4
- resident_ids: int32 [512], replicated, may hold values from 0 to 2047, as said below
- diagonal_shift: float32 [8192], replicated, may hold values from 2 to 4
- background: float32 [8192, 8192], P('row', 'col'), as said below
Outputs:
- dielectric: float32 [8192, 8192], P('row', 'col')
- kernel: float32 [2048, 512], P(('col', 'row'))
Inputs may be any that keep to these rules, and one draw needn't show every extreme that they name: `resident_ids`: 512 distinct pair indices. background is symmetric.
All inputs are finite; a program needn't handle non-finite values.
Results may differ from a plain program's by a relative error of at most 0.0003.
Values may be sent and summed in bfloat16 or wider, within the bound.
No kernel may reach another device: no remote copies, remote signals or barrier semaphores. Data moves between devices by JAX's collectives and lax.ppermute only.
A program may use at most 128 MiB of HBM per device.

v0:
```python
import math
import jax
import jax.numpy as jnp
from jax import lax
from jax.sharding import PartitionSpec as P

NG = 8192
SWEEPS = 2
damping = 0.5


def from_root(block, axis, owner):
    block = jnp.where(lax.axis_index(axis) == owner, block, jnp.zeros_like(block))
    return lax.psum(block, axis)


def scale_factor(exponent):
    return jnp.where(exponent < 0, 0.5, jnp.where(exponent > 0, 2.0, 1.0)).astype(jnp.float32)


def pair_contract(left_block, right_block):
    return lax.dot_general(
        left_block, right_block, (((0,), (0,)), ((), ())), preferred_element_type=jnp.float32
    )


def shards(pair_density, scale_exp, pair_weight, resident_ids, diagonal_shift, background):
    row_count = lax.axis_size("row")
    col_count = lax.axis_size("col")
    row_index = lax.axis_index("row")
    col_index = lax.axis_index("col")
    pair_dev, row_width = pair_density.shape
    col_width = background.shape[1]
    pair_total = pair_dev * col_count
    norm_scale = 4 * pair_total
    factor = scale_factor(scale_exp)
    own_factor = lax.dynamic_slice_in_dim(factor, col_index * pair_dev, pair_dev)
    scaled = (pair_density.astype(jnp.float32) * own_factor[:, None]).astype(jnp.bfloat16)
    left_all = lax.all_gather(scaled, "col", axis=0, tiled=True)
    relaid = lax.all_to_all(
        lax.all_to_all(scaled, "row", split_axis=0, concat_axis=1, tiled=True),
        "col",
        split_axis=1,
        concat_axis=0,
        tiled=True,
    )
    share_rows = pair_dev // row_count
    left_order = left_all.reshape(col_count, row_count, share_rows, row_width)
    left_order = left_order.transpose(1, 0, 2, 3).reshape(pair_total, row_width)
    contracted = pair_contract(left_order, lax.all_gather(relaid, "row", axis=0, tiled=True))
    response = contracted / norm_scale
    row_start = row_index * row_width
    col_start = col_index * col_width
    global_rows = row_start + lax.broadcasted_iota(jnp.int32, (row_width, col_width), 0)
    global_cols = col_start + lax.broadcasted_iota(jnp.int32, (row_width, col_width), 1)
    shift_rows = lax.dynamic_slice_in_dim(diagonal_shift, row_start, row_width)
    dielectric = (
        background + response + jnp.where(global_rows == global_cols, shift_rows[:, None], 0.0)
    )
    precond_rows = (
        shift_rows
        + jnp.einsum("pg,pg->g", left_all, left_all, preferred_element_type=jnp.float32)
        / norm_scale
    )
    picked = left_all[resident_ids].astype(jnp.float32) / factor[resident_ids][:, None]
    source_rows = picked.T
    col_ratio = col_count // row_count
    root_row = col_index // col_ratio
    offset = col_index % col_ratio * col_width

    def column_share(values):
        return lax.dynamic_slice_in_dim(values, offset, col_width, 0)

    source_cols, precond_cols = (
        from_root(column_share(source_rows), "row", root_row),
        from_root(column_share(precond_rows), "row", root_row),
    )
    screen_rows = source_rows / precond_rows[:, None]
    screen_cols = source_cols / precond_cols[:, None]
    for sweep_index in range(SWEEPS):
        last_sweep = sweep_index + 1 == SWEEPS
        row_image = lax.psum(
            jnp.dot(dielectric, screen_cols, precision=lax.Precision.HIGHEST), "col"
        )
        if not last_sweep:
            transposed = lax.dot_general(
                dielectric, screen_rows, (((0,), (0,)), ((), ())), precision=lax.Precision.HIGHEST
            )
            col_image = lax.psum(transposed, "row")
            screen_cols = screen_cols + damping * (source_cols - col_image) / precond_cols[:, None]
        screen_rows = screen_rows + damping * (source_rows - row_image) / precond_rows[:, None]
    partial_value = jnp.dot(
        pair_density.astype(jnp.float32), screen_rows, precision=lax.Precision.HIGHEST
    )
    summed = lax.psum_scatter(partial_value, "row", scatter_dimension=0, tiled=True)
    kernel_share = pair_dev // row_count
    weights = lax.dynamic_slice_in_dim(
        pair_weight, col_index * pair_dev + row_index * kernel_share, kernel_share
    ).astype(jnp.float32)
    kernel = weights[:, None] * summed / math.sqrt(NG)
    return (dielectric, kernel)


def solution(mesh):
    return jax.shard_map(
        shards,
        mesh=mesh,
        in_specs=(P("col", "row"), P(), P(), P(), P(), P("row", "col")),
        out_specs=(P("row", "col"), P(("col", "row"), None)),
        check_vma=False,
    )
```

profile of v0, /device:TPU:0, one launch (start us, length us, event | category | flops | bytes accessed | tf_op | source)
XLA Modules:
  0.0 656.9 jit_solution(1160271850657053020)
XLA Ops:
  8.0 2.4 multiply_convert_fusion
  10.5 18.7 %all_to_all.35 = bf16[4,64,2048]{2,1,0:T(8,128)(2,1)S(1)} all-to-all(bf16[4,64,2048]{2,1,0:T(8,128)(2,1)} %bitcast.38), channel_id=1, replica_groups=mesh['row'=4,'col'=8] {'row'}, dimensions={0} | all-to-all | bytes 2097152 | tf_op jit(solution)/shard_map/all_to_all | solution.py:41
  29.2 0.8 copy.14
  30.9 51.7 %all_to_all.36 = bf16[64,8,1024]{2,0,1:T(8,128)(2,1)} all-to-all(bf16[64,8,1024]{2,0,1:T(8,128)(2,1)S(1)} %copy.15), channel_id=1, replica_groups=mesh['row'=4,'col'=8] {'col'}, dimensions={1} | all-to-all | bytes 2097152 | tf_op jit(solution)/shard_map/all_to_all | solution.py:40
  83.2 3.1 gather_fusion.1
  86.4 72.6 %all-gather.3.cloned.1.call-done = bf16[2048,2048]{1,0:T(8,128)(2,1)} async-done(((bf16[256,2048]{1,0:T(8,128)(2,1)}), bf16[2048,2048]{1,0:T(8,128)(2,1)}) %all-gather.3.cloned.1.call-update) | async-done | bytes 8388624 | tf_op jit(solution)/shard_map/all_gather | solution.py:39
  159.0 9.7 %gather_fusion = bf16[512,2048]{1,0:T(8,128)(2,1)} fusion(bf16[2048,2048]{1,0:T(8,128)(2,1)} %all-gather.3.cloned.1.call-done, s32[1024]{0:T(1024)S(1)} %pad_clamp_fusion), kind=kCustom, calls=%fused_computation | custom fusion | bytes 4196352 | tf_op jit(solution)/shard_map/gather | solution.py:65
  168.7 2.9 copy.16
  171.6 2.6 convert_element_type.25
  174.1 8.5 %copy.13 = bf16[8,4,64,2048]{3,2,0,1:T(8,128)(2,1)} copy(bf16[8,4,64,2048]{3,2,1,0:T(8,128)(2,1)} %bitcast.37) | data formatting | bytes 16777216 | tf_op jit(solution)/shard_map/reshape | solution.py:48
  182.6 5.2 fusion
  188.5 4.8 all-gather.5.cloned.1.call-done
  193.2 15.4 %select_add_fusion = f32[2048,1024]{1,0:T(8,128)S(1)} fusion(f32[2048,1024]{1,0:T(8,128)} %param.11, bf16[2048,2048]{1,0:T(8,128)(2,1)} %bitcast.39, bf16[2048,1024]{1,0:T(8,128)(2,1)} %all-gather.5.cloned.1.call-done, f32[2048]{0:T(1024)S(1)} %get-tuple-element.13, s32[1024]{0:T(1024)S(1)} %iota_add_fusion.1, s32[2048]{0:T(1024)S(1)} %iota_add_fusion), kind=kOutput, calls=%fused_computation.4 | convolution fusion | flops 8600420352 | bytes 29380608 | tf_op jit(solution)/shard_map/dot_general | solution.py:22
  208.6 16.1 %fusion.10 = f32[1024,512]{1,0:T(8,128)} fusion(f32[2048,1024]{1,0:T(8,128)S(1)} %select_add_fusion, bf16[512,2048]{0,1:T(8,128)(2,1)S(1)} %copy.16, f32[2048]{0:T(1024)S(1)} %get-tuple-element.12, f32[512]{0:T(512)S(1)} %gather_fusion.1), kind=kOutput, calls=%fused_computation.16 | convolution fusion | flops 12888047616 | bytes 12593152 | tf_op jit(solution)/shard_map/dot_general | solution.py:86
  224.8 1.6 fusion.12
  226.4 5.9 psum.36
  232.3 79.7 %all-reduce.7.cloned.1.call-done = (f32[1024,512]{1,0:T(8,128)}, f32[1024,512]{1,0:T(8,128)}) async-done(((f32[1024,512]{1,0:T(8,128)}, f32[1024,512]{1,0:T(8,128)}), (f32[1024,512]{1,0:T(8,128)}, f32[1024,512]{1,0:T(8,128)})) %all-reduce.7.cloned.1.call-update) | async-done | bytes 4194320 | tf_op jit(solution)/shard_map/psum | solution.py:14
  312.0 18.0 %fusion.30 = f32[2048,512]{1,0:T(8,128)} fusion(f32[2048,1024]{1,0:T(8,128)} %copy-done.5, f32[1024,512]{1,0:T(8,128)} %get-tuple-element.10, f32[1024]{0:T(1024)S(1)} %psum.36), kind=kOutput, calls=%fused_computation.37 | convolution fusion | flops 12885426176 | bytes 14684160 | tf_op jit(solution)/shard_map/dot_general | solution.py:83
  330.0 15.5 %fusion.15 = f32[2048,512]{1,0:T(8,128)} fusion(f32[2048,1024]{1,0:T(8,128)S(1)} %copy-done.6, f32[1024,512]{1,0:T(8,128)S(1)} %copy-done.3, f32[1024,512]{1,0:T(8,128)S(1)} %copy-done.4, f32[1024]{0:T(1024)S(1)} %psum.36), kind=kOutput, calls=%fused_computation.22 | convolution fusion | flops 12887523328 | bytes 16781312 | tf_op jit(solution)/shard_map/dot_general | solution.py:83
  345.8 270.0 %all-reduce.5.cloned.1.call-done = (f32[2048,512]{1,0:T(8,128)}, f32[2048,512]{1,0:T(8,128)}) async-done(((f32[2048,512]{1,0:T(8,128)}, f32[2048,512]{1,0:T(8,128)}), (f32[2048,512]{1,0:T(8,128)}, f32[2048,512]{1,0:T(8,128)})) %all-reduce.5.cloned.1.call-update) | async-done | bytes 8388624 | tf_op jit(solution)/shard_map/psum | solution.py:82
  615.9 9.4 %fusion.25 = f32[256,512]{0,1:T(8,128)} fusion(bf16[256,2048]{1,0:T(8,128)(2,1)S(1)} %copy-done.1, f32[2048,512]{1,0:T(8,128)} %get-tuple-element.8, f32[2048,512]{1,0:T(8,128)} %get-tuple-element.9, bf16[512,2048]{0,1:T(8,128)(2,1)S(1)} %copy.16, f32[2048]{0:T(1024)S(1)} %get-tuple-element.12, f32[512]{0:T(512)S(1)} %gather_fusion.1), kind=kOutput, calls=%fused_computation.33 | convolution fusion | flops 3233808384 | bytes 12068864 | tf_op jit(solution)/shard_map/dot_general | solution.py:92
  625.3 2.0 copy.24
  628.1 20.1 %reduce-scatter.4.cloned.1.call-done = f32[64,512]{1,0:T(8,128)} async-done(((f32[256,512]{1,0:T(8,128)}), f32[64,512]{1,0:T(8,128)}) %reduce-scatter.4.cloned.1.call-update) | async-done | bytes 131088
  648.3 1.0 copy.25
  (37 shorter events, 5.0 us)
Async XLA Ops:
  7.2 151.8 %all-gather.3.cloned.1.call-start = ((), (), s32[]{:S(2)}) async-start(), calls=%async_computation.3 | async-start | bytes 9437184 | tf_op jit(solution)/shard_map/all_gather | solution.py:39
  10.4 182.8 %all-gather.5.cloned.1.call-start = ((), (), s32[]{:S(2)}) async-start(), calls=%async_computation.4 | async-start | bytes 5242880 | tf_op jit(solution)/shard_map/all_gather | solution.py:50
  30.0 53.2 %copy-start.2 = (s32[512]{0:T(512)S(1)}, s32[512]{0:T(512)}, u32[]{:S(2)}) copy-start(s32[512]{0:T(512)} %param.9) | copy-start | bytes 6148
  82.6 229.5 %all-reduce.7.cloned.1.call-start = ((), (), s32[]{:S(2)}) async-start(), calls=%async_computation.7 | async-start | bytes 8388608 | tf_op jit(solution)/shard_map/psum | solution.py:14
  208.6 16.1 %copy-start.5 = (f32[2048,1024]{1,0:T(8,128)}, f32[2048,1024]{1,0:T(8,128)S(1)}, u32[]{:S(2)}) copy-start(f32[2048,1024]{1,0:T(8,128)S(1)} %select_add_fusion) | copy-start | bytes 25165828
  208.6 16.1 %copy-start = (f32[512,2048]{0,1:T(8,128)S(1)}, f32[512,2048]{0,1:T(8,128)}, u32[]{:S(2)}) copy-start(f32[512,2048]{0,1:T(8,128)} %convert_element_type.25) | copy-start | bytes 12582916
  226.4 389.5 %all-reduce.5.cloned.1.call-start = ((), (), s32[]{:S(2)}) async-start(), calls=%async_computation.6 | async-start | bytes 16777216 | tf_op jit(solution)/shard_map/psum | solution.py:82
  312.0 18.0 %copy-start.3 = (f32[1024,512]{1,0:T(8,128)S(1)}, f32[1024,512]{1,0:T(8,128)}, u32[]{:S(2)}) copy-start(f32[1024,512]{1,0:T(8,128)} %get-tuple-element.10) | copy-start | bytes 6291460
  312.0 18.0 %copy-start.4 = (f32[1024,512]{1,0:T(8,128)S(1)}, f32[1024,512]{1,0:T(8,128)}, u32[]{:S(2)}) copy-start(f32[1024,512]{1,0:T(8,128)} %get-tuple-element.11) | copy-start | bytes 6291460
  312.0 18.0 %copy-start.6 = (f32[2048,1024]{1,0:T(8,128)S(1)}, f32[2048,1024]{1,0:T(8,128)}, u32[]{:S(2)}) copy-start(f32[2048,1024]{1,0:T(8,128)} %copy-done.5) | copy-start | bytes 25165828
  345.5 270.4 %copy-start.1 = (bf16[256,2048]{1,0:T(8,128)(2,1)S(1)}, bf16[256,2048]{1,0:T(8,128)(2,1)}, u32[]{:S(2)}) copy-start(bf16[256,2048]{1,0:T(8,128)(2,1)} %param.6) | copy-start | bytes 3145732
  345.5 302.7 %reduce-scatter.4.cloned.1.call-start = ((), (), s32[]{:S(2)}) async-start(), calls=%async_computation.5 | async-start | bytes 655360
Sparse Core Ops, SparseCore 0:
  10.7 148.2 all-gather.2
  160.6 32.6 all-gather.4
  226.5 85.5 all-reduce.6
  345.6 270.1 all-reduce.4
  627.5 20.7 reduce-scatter.3
where the time goes:
time: 660 us; the launch traced here: 657 us
  waiting for transfers between devices  447 us (68%)
  blocking collectives  76.2 us (12%)
  matrix products  74.4 us (11%)
  local copies, waits for them, and re-layouts  29.8 us (5%)
  between operations  14.2 us (2%)
  other arithmetic  13.9 us (2%)
    psum x1, waiting for transfers between devices, shards(): lax.psum(jnp.dot(dielectric, screen_cols, precision=lax.Precision.HIGHEST...  270 us
    psum x1, waiting for transfers between devices, from_root(): return lax.psum(block, axis)  79.7 us
    all_gather x1, waiting for transfers between devices, shards(): left_all = lax.all_gather(scaled, 'col', axis=0, tiled=True)  72.6 us
    all_to_all x1, blocking collectives, shards(): lax.all_to_all(lax.all_to_all(scaled, 'row', split_axis=0, concat_axis=1,...  51.7 us
    dot_general x2, matrix products, shards(): jnp.dot(dielectric, screen_cols, precision=lax.Precision.HIGHEST)  33.4 us
    unnamed x6, waiting for transfers between devices  20.2 us
    all_to_all x1, blocking collectives, shards(): lax.all_to_all(scaled, 'row', split_axis=0, concat_axis=1, tiled=True)  18.7 us
    dot_general x1, matrix products, shards(): lax.dot_general(dielectric, screen_rows, (((0,), (0,)), ((), ())), precis...  16.1 us
  transfers between devices with their start and end apart: 5, of which 5 were waited for; matrix products, arithmetic and copies ran while one was open for 5% of the time, Pallas kernels for 0%

commit v1 on v0

--- a/solution.py
+++ b/solution.py
@@ -36,7 +36,23 @@
     factor = scale_factor(scale_exp)
     own_factor = lax.dynamic_slice_in_dim(factor, col_index * pair_dev, pair_dev)
     scaled = (pair_density.astype(jnp.float32) * own_factor[:, None]).astype(jnp.bfloat16)
-    left_all = lax.all_gather(scaled, "col", axis=0, tiled=True)
+
+    def packet_settle(unit, comm_axis):
+        fan = lax.axis_size(comm_axis)
+        out_arr = [(t - 1, t) for t in range(1, fan)] + [(fan - 1, 0)]
+        z_new = unit
+        arrivals = [z_new]
+        for _ in range(fan - 1):
+            z_new = lax.ppermute(z_new, comm_axis, perm=out_arr)
+            arrivals += [z_new]
+        all_values = jnp.roll(
+            jnp.concatenate([*reversed(arrivals)], axis=0),
+            (lax.axis_index(comm_axis) + 1) * z_new.shape[0],
+            axis=0,
+        )
+        return all_values
+
+    left_all = packet_settle(scaled, "col")
     relaid = lax.all_to_all(
         lax.all_to_all(scaled, "row", split_axis=0, concat_axis=1, tiled=True),
         "col",

time: 660 us -> 744 us (1.13)
  waiting for transfers between devices: 447 us -> 543 us
  blocking collectives: 76.2 us -> 5.67 us
  local copies, waits for them, and re-layouts: 29.8 us -> 67.2 us
  starting transfers between devices: 0.98 us -> 16.7 us
    ppermute x0 -> x7, waiting for transfers between devices: none -> 169 us  [packet_settle(): z_new = lax.ppermute(z_new, comm_axis, perm=out_arr)]
    all_gather x1 -> x0, waiting for transfers between devices: 72.6 us -> none  [shards(): left_all = lax.all_gather(scaled, 'col', axis=0, tiled=True)]
    all_to_all x2 -> x0, blocking collectives: 70.3 us -> none  [the longest x1 51.7 us: shards(): lax.all_to_all(lax.all_to_all(scaled, 'row', split_axis=0, concat_axis=1,...]
    unnamed x17 -> x31, local copies, waits for them, and re-layouts: 3.87 us -> 35.1 us
    all_to_all x0 -> x2, starting transfers between devices: none -> 10.2 us  [the longest x1 6 us: shards(): lax.all_to_all(lax.all_to_all(scaled, 'row', split_axis=0, concat_axis=1,...]
    reshape x1 -> x0, local copies, waits for them, and re-layouts: 8.48 us -> none  [shards(): left_order = left_all.reshape(col_count, row_count, share_rows, row_width)]
    transpose x0 -> x1, local copies, waits for them, and re-layouts: none -> 8.29 us  [shards(): left_order = left_order.transpose(1, 0, 2, 3).reshape(pair_total, row_width)]
    unnamed x6 -> x5, waiting for transfers between devices: 20.2 us -> 20.2 us
  transfers between devices with their start and end apart: 5 -> 13, of which waited for: 5 -> 10; matrix products, arithmetic and copies ran while one was open for 5% -> 10% of each run, Pallas kernels for 0% -> 0%
where the time goes in v1:
time: 744 us; the launch traced here: 740 us
  waiting for transfers between devices  543 us (73%)
  matrix products  74.4 us (10%)
  local copies, waits for them, and re-layouts  67.2 us (9%)
  other arithmetic  18.6 us (3%)
  starting transfers between devices  16.7 us (2%)
  between operations  14.4 us (2%)
    psum x1, waiting for transfers between devices, shards(): lax.psum(jnp.dot(dielectric, screen_cols, precision=lax.Precision.HIGHEST...  270 us
    ppermute x7, waiting for transfers between devices, packet_settle(): z_new = lax.ppermute(z_new, comm_axis, perm=out_arr)  169 us
    psum x1, waiting for transfers between devices, from_root(): return lax.psum(block, axis)  84.5 us
    unnamed x31, local copies, waits for them, and re-layouts  35.1 us
    dot_general x2, matrix products, shards(): jnp.dot(dielectric, screen_cols, precision=lax.Precision.HIGHEST)  33.5 us
    unnamed x5, waiting for transfers between devices  20.2 us
    dot_general x1, matrix products, shards(): lax.dot_general(dielectric, screen_rows, (((0,), (0,)), ((), ())), precis...  16.1 us
    dot_general x1, matrix products, pair_contract(): lax.dot_general(left_block, right_block, (((0,), (0,)), ((), ())), prefer...  15.4 us
  transfers between devices with their start and end apart: 13, of which 10 were waited for; matrix products, arithmetic and copies ran while one was open for 10% of the time, Pallas kernels for 0%

profile of v1, /device:TPU:0, one launch (start us, length us, event | category | flops | bytes accessed | tf_op | source)
XLA Modules:
  0.0 740.3 jit_solution(437090732018930095)
XLA Ops:
  9.4 3.0 collective-permute-start
  12.5 26.2 %collective-permute-done = bf16[256,2048]{1,0:T(8,128)(2,1)S(1)} collective-permute-done((bf16[256,2048]{1,0:T(8,128)(2,1)S(1)}, bf16[256,2048]{1,0:T(8,128)(2,1)S(1)}, u32[]{:S(2)}, u32[]{:S(2)}) %collective-permute-start) | collective-permute-done | bytes 1048608 | tf_op jit(solution)/shard_map/ppermute | solution.py:46
  38.7 27.0 %collective-permute-done.1 = bf16[256,2048]{1,0:T(8,128)(2,1)S(1)} collective-permute-done((bf16[256,2048]{1,0:T(8,128)(2,1)S(1)}, bf16[256,2048]{1,0:T(8,128)(2,1)S(1)}, u32[]{:S(2)}, u32[]{:S(2)}) %collective-permute-start.1) | collective-permute-done | bytes 1048608 | tf_op jit(solution)/shard_map/ppermute | solution.py:46
  65.7 26.3 %collective-permute-done.2 = bf16[256,2048]{1,0:T(8,128)(2,1)} collective-permute-done((bf16[256,2048]{1,0:T(8,128)(2,1)S(1)}, bf16[256,2048]{1,0:T(8,128)(2,1)}, u32[]{:S(2)}, u32[]{:S(2)}) %collective-permute-start.2) | collective-permute-done | bytes 1048608 | tf_op jit(solution)/shard_map/ppermute | solution.py:46
  92.0 4.2 all-to-all-start
  96.2 21.4 %collective-permute-done.3 = bf16[256,2048]{1,0:T(8,128)(2,1)} collective-permute-done((bf16[256,2048]{1,0:T(8,128)(2,1)}, bf16[256,2048]{1,0:T(8,128)(2,1)}, u32[]{:S(2)}, u32[]{:S(2)}) %collective-permute-start.3) | collective-permute-done | bytes 1048608 | tf_op jit(solution)/shard_map/ppermute | solution.py:46
  125.5 6.0 all-to-all-start.1
  131.6 16.9 %collective-permute-done.4 = bf16[256,2048]{1,0:T(8,128)(2,1)} collective-permute-done((bf16[256,2048]{1,0:T(8,128)(2,1)}, bf16[256,2048]{1,0:T(8,128)(2,1)}, u32[]{:S(2)}, u32[]{:S(2)}) %collective-permute-start.4) | collective-permute-done | bytes 1048608 | tf_op jit(solution)/shard_map/ppermute | solution.py:46
  151.0 30.8 %collective-permute-done.5 = bf16[256,2048]{1,0:T(8,128)(2,1)} collective-permute-done((bf16[256,2048]{1,0:T(8,128)(2,1)}, bf16[256,2048]{1,0:T(8,128)(2,1)}, u32[]{:S(2)}, u32[]{:S(2)}) %collective-permute-start.5) | collective-permute-done | bytes 1048608 | tf_op jit(solution)/shard_map/ppermute | solution.py:46
  182.4 3.1 gather_fusion.1
  185.7 20.1 %collective-permute-done.6 = bf16[256,2048]{1,0:T(8,128)(2,1)} collective-permute-done((bf16[256,2048]{1,0:T(8,128)(2,1)}, bf16[256,2048]{1,0:T(8,128)(2,1)}, u32[]{:S(2)}, u32[]{:S(2)}) %collective-permute-start.6) | collective-permute-done | bytes 1048608 | tf_op jit(solution)/shard_map/ppermute | solution.py:46
  236.2 10.2 %fusion = (f32[2048]{0:T(1024)S(1)}, bf16[2048,2048]{1,0:T(8,128)(2,1)}) fusion(bf16[4096,2048]{1,0:T(8,128)(2,1)} %constant_dynamic-update-slice_fusion, s32[]{:T(128)S(6)} %select_n.75), kind=kLoop, calls=%fused_computation.3 | loop fusion | flops 12580864 | bytes 16785412 | tf_op jit(solution)/shard_map/pg,pg->g/dot_general | solution.py:78
  246.4 9.7 %gather_fusion = bf16[512,2048]{1,0:T(8,128)(2,1)} fusion(bf16[2048,2048]{1,0:T(8,128)(2,1)} %get-tuple-element.17, s32[1024]{0:T(1024)S(1)} %pad_clamp_fusion), kind=kCustom, calls=%fused_computation | custom fusion | bytes 4196352 | tf_op jit(solution)/shard_map/gather | solution.py:81
  256.1 8.3 %copy.17 = bf16[4,8,64,2048]{3,2,1,0:T(8,128)(2,1)} copy(bf16[4,8,64,2048]{3,2,0,1:T(8,128)(2,1)} %bitcast.37) | data formatting | bytes 16777216 | tf_op jit(solution)/shard_map/transpose | solution.py:65
  270.2 15.4 %select_add_fusion = f32[2048,1024]{1,0:T(8,128)S(1)} fusion(f32[2048,1024]{1,0:T(8,128)} %param.11, bf16[2048,2048]{1,0:T(8,128)(2,1)} %bitcast.38, bf16[2048,1024]{1,0:T(8,128)(2,1)} %all-gather.2.cloned.1.call-done, f32[2048]{0:T(1024)S(1)} %get-tuple-element.15, s32[1024]{0:T(1024)S(1)} %iota_add_fusion.1, s32[2048]{0:T(1024)S(1)} %iota_add_fusion), kind=kOutput, calls=%fused_computation.4 | convolution fusion | flops 8600420352 | bytes 29380608 | tf_op jit(solution)/shard_map/dot_general | solution.py:22
  285.6 3.4 copy-done.5
  289.0 16.1 %fusion.10 = f32[1024,512]{1,0:T(8,128)} fusion(f32[2048,1024]{1,0:T(8,128)S(1)} %select_add_fusion, bf16[512,2048]{0,1:T(8,128)(2,1)S(1)} %copy.20, f32[2048]{0:T(1024)S(1)} %get-tuple-element.14, f32[512]{0:T(512)S(1)} %gather_fusion.1), kind=kOutput, calls=%fused_computation.16 | convolution fusion | flops 12888047616 | bytes 12593152 | tf_op jit(solution)/shard_map/dot_general | solution.py:102
  305.2 5.7 psum.36
  310.8 84.5 %all-reduce.7.cloned.1.call-done = (f32[1024,512]{1,0:T(8,128)}, f32[1024,512]{1,0:T(8,128)}) async-done(((f32[1024,512]{1,0:T(8,128)}, f32[1024,512]{1,0:T(8,128)}), (f32[1024,512]{1,0:T(8,128)}, f32[1024,512]{1,0:T(8,128)})) %all-reduce.7.cloned.1.call-update) | async-done | bytes 4194320 | tf_op jit(solution)/shard_map/psum | solution.py:14
  395.3 18.0 %fusion.30 = f32[2048,512]{1,0:T(8,128)} fusion(f32[2048,1024]{1,0:T(8,128)} %copy-done.5, f32[1024,512]{1,0:T(8,128)} %get-tuple-element.12, f32[1024]{0:T(1024)S(1)} %psum.36), kind=kOutput, calls=%fused_computation.37 | convolution fusion | flops 12885426176 | bytes 14684160 | tf_op jit(solution)/shard_map/dot_general | solution.py:99
  413.3 15.5 %fusion.15 = f32[2048,512]{1,0:T(8,128)} fusion(f32[2048,1024]{1,0:T(8,128)S(1)} %copy-done.6, f32[1024,512]{1,0:T(8,128)S(1)} %copy-done.3, f32[1024,512]{1,0:T(8,128)S(1)} %copy-done.4, f32[1024]{0:T(1024)S(1)} %psum.36), kind=kOutput, calls=%fused_computation.22 | convolution fusion | flops 12887523328 | bytes 16781312 | tf_op jit(solution)/shard_map/dot_general | solution.py:99
  429.1 270.0 %all-reduce.5.cloned.1.call-done = (f32[2048,512]{1,0:T(8,128)}, f32[2048,512]{1,0:T(8,128)}) async-done(((f32[2048,512]{1,0:T(8,128)}, f32[2048,512]{1,0:T(8,128)}), (f32[2048,512]{1,0:T(8,128)}, f32[2048,512]{1,0:T(8,128)})) %all-reduce.5.cloned.1.call-update) | async-done | bytes 8388624 | tf_op jit(solution)/shard_map/psum | solution.py:98
  699.1 9.4 %fusion.25 = f32[256,512]{0,1:T(8,128)} fusion(bf16[256,2048]{1,0:T(8,128)(2,1)S(1)} %copy-done, f32[2048,512]{1,0:T(8,128)} %get-tuple-element.10, f32[2048,512]{1,0:T(8,128)} %get-tuple-element.11, bf16[512,2048]{0,1:T(8,128)(2,1)S(1)} %copy.20, f32[2048]{0:T(1024)S(1)} %get-tuple-element.14, f32[512]{0:T(512)S(1)} %gather_fusion.1), kind=kOutput, calls=%fused_computation.33 | convolution fusion | flops 3233808384 | bytes 12068864 | tf_op jit(solution)/shard_map/dot_general | solution.py:108
  711.4 20.1 %reduce-scatter.4.cloned.1.call-done = f32[64,512]{1,0:T(8,128)} async-done(((f32[256,512]{1,0:T(8,128)}), f32[64,512]{1,0:T(8,128)}) %reduce-scatter.4.cloned.1.call-update) | async-done | bytes 131088
  (66 shorter events, 54.6 us)
Async XLA Ops:
  9.4 82.6 %copy-start.1 = (bf16[256,2048]{1,0:T(8,128)(2,1)}, bf16[256,2048]{1,0:T(8,128)(2,1)S(1)}, u32[]{:S(2)}) copy-start(bf16[256,2048]{1,0:T(8,128)(2,1)S(1)} %multiply_convert_fusion) | copy-start | bytes 3145732
  9.4 29.2 %collective-permute-start = (bf16[256,2048]{1,0:T(8,128)(2,1)S(1)}, bf16[256,2048]{1,0:T(8,128)(2,1)S(1)}, u32[]{:S(2)}, u32[]{:S(2)}) collective-permute-start(bf16[256,2048]{1,0:T(8,128)(2,1)S(1)} %multiply_convert_fusion), channel_id=1, source_target_pairs={{0,1},{1,2},{2,3},{3,4},{4,5},{5,6},{6,7},{7,0},{8,9},{9,10},{10,1... | collective-permute-start | bytes 3145736 | tf_op jit(solution)/shard_map/ppermute | solution.py:46
  38.7 27.0 %collective-permute-start.1 = (bf16[256,2048]{1,0:T(8,128)(2,1)S(1)}, bf16[256,2048]{1,0:T(8,128)(2,1)S(1)}, u32[]{:S(2)}, u32[]{:S(2)}) collective-permute-start(bf16[256,2048]{1,0:T(8,128)(2,1)S(1)} %collective-permute-done), channel_id=1, source_target_pairs={{0,1},{1,2},{2,3},{3,4},{4,5},{5,6},{6,7},{7,0},{8,9},{9,10},{10,1... | collective-permute-start | bytes 3145736 | tf_op jit(solution)/shard_map/ppermute | solution.py:46
  65.7 26.3 %collective-permute-start.2 = (bf16[256,2048]{1,0:T(8,128)(2,1)S(1)}, bf16[256,2048]{1,0:T(8,128)(2,1)}, u32[]{:S(2)}, u32[]{:S(2)}) collective-permute-start(bf16[256,2048]{1,0:T(8,128)(2,1)S(1)} %collective-permute-done.1), channel_id=1, source_target_pairs={{0,1},{1,2},{2,3},{3,4},{4,5},{5,6},{6,7},{7,0},{8,9},{9,10},{10,1... | collective-permute-start | bytes 3145736 | tf_op jit(solution)/shard_map/ppermute | solution.py:46
  92.0 25.6 %collective-permute-start.3 = (bf16[256,2048]{1,0:T(8,128)(2,1)}, bf16[256,2048]{1,0:T(8,128)(2,1)}, u32[]{:S(2)}, u32[]{:S(2)}) collective-permute-start(bf16[256,2048]{1,0:T(8,128)(2,1)} %collective-permute-done.2), channel_id=1, source_target_pairs={{0,1},{1,2},{2,3},{3,4},{4,5},{5,6},{6,7},{7,0},{8,9},{9,10},{10,1... | collective-permute-start | bytes 3145736 | tf_op jit(solution)/shard_map/ppermute | solution.py:46
  92.0 25.6 %all-to-all-start = ((bf16[4,64,2048]{2,1,0:T(8,128)(2,1)}), bf16[4,64,2048]{2,1,0:T(8,128)(2,1)}, u32[]{:S(2)}, u32[]{:S(2)}) async-start(bf16[4,64,2048]{2,1,0:T(8,128)(2,1)} %bitcast.39), calls=%async_computation | async-start | bytes 2097152 | tf_op jit(solution)/shard_map/all_to_all | solution.py:57
  117.6 30.9 %collective-permute-start.4 = (bf16[256,2048]{1,0:T(8,128)(2,1)}, bf16[256,2048]{1,0:T(8,128)(2,1)}, u32[]{:S(2)}, u32[]{:S(2)}) collective-permute-start(bf16[256,2048]{1,0:T(8,128)(2,1)} %collective-permute-done.3), channel_id=1, source_target_pairs={{0,1},{1,2},{2,3},{3,4},{4,5},{5,6},{6,7},{7,0},{8,9},{9,10},{10,1... | collective-permute-start | bytes 3145736 | tf_op jit(solution)/shard_map/ppermute | solution.py:46
  120.6 61.8 %copy-start.2 = (s32[512]{0:T(512)S(1)}, s32[512]{0:T(512)}, u32[]{:S(2)}) copy-start(s32[512]{0:T(512)} %param.9) | copy-start | bytes 6148
  125.5 56.2 %all-to-all-start.1 = ((bf16[64,8,1024]{2,0,1:T(8,128)(2,1)}), bf16[64,8,1024]{2,0,1:T(8,128)(2,1)}, u32[]{:S(2)}, u32[]{:S(2)}) async-start(bf16[64,8,1024]{2,0,1:T(8,128)(2,1)} %copy.19), calls=%async_computation.1 | async-start | bytes 2097152 | tf_op jit(solution)/shard_map/all_to_all | solution.py:56
  131.5 138.6 %all-gather.2.cloned.1.call-start = ((), (), s32[]{:S(2)}) async-start(), calls=%async_computation.3 | async-start | bytes 5242880 | tf_op jit(solution)/shard_map/all_gather | solution.py:66
  148.5 33.3 %collective-permute-start.5 = (bf16[256,2048]{1,0:T(8,128)(2,1)}, bf16[256,2048]{1,0:T(8,128)(2,1)}, u32[]{:S(2)}, u32[]{:S(2)}) collective-permute-start(bf16[256,2048]{1,0:T(8,128)(2,1)} %collective-permute-done.4), channel_id=1, source_target_pairs={{0,1},{1,2},{2,3},{3,4},{4,5},{5,6},{6,7},{7,0},{8,9},{9,10},{10,1... | collective-permute-start | bytes 3145736 | tf_op jit(solution)/shard_map/ppermute | solution.py:46
  181.8 24.0 %collective-permute-start.6 = (bf16[256,2048]{1,0:T(8,128)(2,1)}, bf16[256,2048]{1,0:T(8,128)(2,1)}, u32[]{:S(2)}, u32[]{:S(2)}) collective-permute-start(bf16[256,2048]{1,0:T(8,128)(2,1)} %collective-permute-done.5), channel_id=1, source_target_pairs={{0,1},{1,2},{2,3},{3,4},{4,5},{5,6},{6,7},{7,0},{8,9},{9,10},{10,1... | collective-permute-start | bytes 3145736 | tf_op jit(solution)/shard_map/ppermute | solution.py:46
  181.8 213.5 %all-reduce.7.cloned.1.call-start = ((), (), s32[]{:S(2)}) async-start(), calls=%async_computation.6 | async-start | bytes 8388608 | tf_op jit(solution)/shard_map/psum | solution.py:14
  212.7 7.1 copy-start
  285.6 3.4 copy-start.5
  305.1 394.0 %all-reduce.5.cloned.1.call-start = ((), (), s32[]{:S(2)}) async-start(), calls=%async_computation.5 | async-start | bytes 16777216 | tf_op jit(solution)/shard_map/psum | solution.py:98
  395.3 18.0 %copy-start.3 = (f32[1024,512]{1,0:T(8,128)S(1)}, f32[1024,512]{1,0:T(8,128)}, u32[]{:S(2)}) copy-start(f32[1024,512]{1,0:T(8,128)} %get-tuple-element.12) | copy-start | bytes 6291460
  395.3 18.0 %copy-start.4 = (f32[1024,512]{1,0:T(8,128)S(1)}, f32[1024,512]{1,0:T(8,128)}, u32[]{:S(2)}) copy-start(f32[1024,512]{1,0:T(8,128)} %get-tuple-element.13) | copy-start | bytes 6291460
  395.3 18.0 %copy-start.6 = (f32[2048,1024]{1,0:T(8,128)S(1)}, f32[2048,1024]{1,0:T(8,128)}, u32[]{:S(2)}) copy-start(f32[2048,1024]{1,0:T(8,128)} %copy-done.5) | copy-start | bytes 25165828
  428.8 302.7 %reduce-scatter.4.cloned.1.call-start = ((), (), s32[]{:S(2)}) async-start(), calls=%async_computation.4 | async-start | bytes 655360
Sparse Core Ops, SparseCore 0:
  181.9 59.2 all-gather.1
  305.2 90.0 all-reduce.6
  428.9 270.1 all-reduce.4
  710.7 20.7 reduce-scatter.3
